TPU v7x, 32 devices: a whole 2x2x4 slice. The times are simulated.
32 devices in a mesh: dp: 8 (over z, y), tensor: 4 (over x, core).
Axes of the slice: x: 2, y: 2, z: 4, core: 2. Of those that a mesh axis runs over, the one named last changes fastest.
Arguments:
- tokens: bfloat16 [1024, 2048], P('dp'), may hold values from -6 to 6
- lengths: int32 [8], replicated, may hold values from 96 to 128, as said below
- request_adapter: int32 [8], replicated, may hold values from 0 to 63
- token_experts: int32 [1024, 8], P('dp'), may hold values from 0 to 63, as said below
- router_weight: float32 [1024, 8], P('dp'), may hold values from 0.05 to 1
- gate_weight: bfloat16 [128, 2048, 512], P('dp', None, 'tensor'), may hold values from -0.125 to 0.125
- up_weight: bfloat16 [128, 2048, 512], P('dp', None, 'tensor'), may hold values from -0.125 to 0.125
- down_weight: bfloat16 [128, 2048, 512], P('dp', None, 'tensor'), may hold values from -0.1875 to 0.1875
- adapter_input_maps: bfloat16 [2048, 2048], P('tensor', 'dp'), may hold values from -0.125 to 0.125
- adapter_output_maps: bfloat16 [2048, 2, 512], P('dp', None, 'tensor'), may hold values from -1.5 to 1.5
Outputs:
- moe_output: bfloat16 [1024, 2048], P('dp', 'tensor')
Inputs may be any that keep to these rules, and one draw needn't show every extreme that they name: `token_experts`: each row names 8 different experts. Among the rows of one request window, each expert is named by at most 28 rows, and one expert, the same in every window, is named by exactly 28 rows, all of live tokens. `lengths`: some request has all 128 tokens live.
All inputs are finite; a program needn't handle non-finite values.
Results may differ from a plain program's by a relative error of at most 0.0065.
Values may be sent and summed in bfloat16 or wider, within the bound.
No kernel may reach another device: no remote copies, remote signals or barrier semaphores. Data moves between devices by JAX's collectives and lax.ppermute only.
A program may use at most 320 MiB of HBM per device.

v0:
```python
import jax
import jax.numpy as jnp
from jax import lax
from jax.sharding import PartitionSpec as P

ADAPTER_RANK = 16
CAP = 28


def combine_routes(unit_table, lower_slot, shift_half, route_gain, tok_rows, topk):
    lower_slot = lower_slot.reshape(tok_rows, topk)
    route_gain = route_gain.reshape(tok_rows, topk)
    pair_slots = jnp.stack([lower_slot, lower_slot + shift_half], axis=2)
    pair_rows = unit_table[pair_slots].astype(jnp.float32)
    summed_pair = jnp.sum(pair_rows, axis=2)
    return jnp.sum(summed_pair * route_gain[:, :, None], axis=1)


def per_device(
    tokens,
    lengths,
    request_adapter,
    token_experts,
    router_weight,
    gate_weight,
    up_weight,
    down_weight,
    adapter_input_maps,
    adapter_output_maps,
):
    tok_rows, width = tokens.shape
    topk = token_experts.shape[1]
    dp_count = lax.axis_size("dp")
    tp_count = lax.axis_size("tensor")
    units_local = gate_weight.shape[0]
    experts_all = units_local * dp_count // 2
    quarter = CAP // tp_count
    double_rank = 2 * ADAPTER_RANK
    row_index = lax.axis_index("dp")
    part_index = lax.axis_index("tensor")
    live_mask = jnp.arange(tok_rows) < lengths[row_index]
    adapter = request_adapter[row_index]
    width_part = width // tp_count
    x_part = lax.dynamic_slice_in_dim(tokens, part_index * width_part, width_part, 1)
    device_portion = lax.all_gather(adapter_input_maps, "dp", axis=1, tiled=True)
    columns = jnp.arange(device_portion.shape[1])
    selector = (
        columns[:, None] == adapter * double_rank + jnp.arange(double_rank)[None, :]
    ).astype(jnp.bfloat16)
    chosen = jnp.dot(device_portion, selector, preferred_element_type=jnp.float32)
    partial_z = jnp.dot(x_part, chosen.astype(jnp.bfloat16), preferred_element_type=jnp.float32)
    low_rank = lax.psum(partial_z, "tensor").astype(jnp.bfloat16)
    entries = tok_rows * topk
    flat_ids = token_experts.reshape(entries)
    entry_token = jnp.arange(entries) // topk
    entry_live = live_mask[entry_token]
    expert_hits = (
        (flat_ids[:, None] == jnp.arange(experts_all)[None, :]) & entry_live[:, None]
    ).astype(jnp.int32)
    position = jnp.sum(jnp.cumsum(expert_hits, axis=0) * expert_hits, axis=1) - 1
    entry_mine = entry_live & (position // quarter == part_index)
    empty_slot = experts_all * quarter
    slot_part = jnp.where(entry_mine, flat_ids * quarter + position % quarter, empty_slot)
    slot_token = (
        jnp.full((empty_slot + 1,), tok_rows, jnp.int32).at[slot_part].set(entry_token)[:empty_slot]
    )
    padded_x = jnp.concatenate([tokens, jnp.zeros((1, width), jnp.bfloat16)], axis=0)
    padded_z = jnp.concatenate([low_rank, jnp.zeros((1, double_rank), jnp.bfloat16)], axis=0)
    slot_rows = padded_x[slot_token]
    slot_low = padded_z[slot_token]
    send_rows = jnp.concatenate([slot_rows, slot_rows], axis=0).reshape(
        dp_count, units_local, quarter, width
    )
    send_low = jnp.concatenate([slot_low, slot_low], axis=0).reshape(
        dp_count, units_local, quarter, double_rank
    )
    recv_rows, recv_low = (
        lax.all_to_all(send_rows, "dp", split_axis=0, concat_axis=0, tiled=True),
        lax.all_to_all(send_low, "dp", split_axis=0, concat_axis=0, tiled=True),
    )
    every_table = lax.all_gather(adapter_output_maps, "dp", axis=0, tiled=True)
    unit_half = (row_index * units_local + jnp.arange(units_local)) // experts_all
    half_tables = jnp.moveaxis(jnp.take(every_table, unit_half, axis=1), 1, 0)
    source_rows = (
        request_adapter[:, None] * double_rank + jnp.arange(double_rank)[None, :]
    ).reshape(dp_count * double_rank)
    source_tables = jnp.take(half_tables, source_rows, axis=1)
    gate_piece = lax.all_gather(gate_weight, "tensor", axis=2, tiled=True)
    up_piece = lax.all_gather(up_weight, "tensor", axis=2, tiled=True)
    table_piece = lax.all_gather(source_tables, "tensor", axis=2, tiled=True)
    table_split = table_piece.reshape(units_local, dp_count, double_rank, table_piece.shape[2])
    gate_term = jnp.einsum(
        "slcd,ldk->slck", recv_rows, gate_piece, preferred_element_type=jnp.float32
    )
    gate_term = gate_term + jnp.einsum(
        "slcj,lsjk->slck",
        recv_low[..., :ADAPTER_RANK],
        table_split[:, :, :ADAPTER_RANK],
        preferred_element_type=jnp.float32,
    )
    up_term = jnp.einsum("slcd,ldk->slck", recv_rows, up_piece, preferred_element_type=jnp.float32)
    up_term = up_term + jnp.einsum(
        "slcj,lsjk->slck",
        recv_low[..., ADAPTER_RANK:],
        table_split[:, :, ADAPTER_RANK:],
        preferred_element_type=jnp.float32,
    )
    hidden = (jax.nn.silu(gate_term) * up_term).astype(jnp.bfloat16)
    down_whole = lax.all_gather(down_weight, "tensor", axis=2, tiled=True)
    unit_output = jnp.einsum(
        "slck,ldk->slcd", hidden, down_whole, preferred_element_type=jnp.float32
    ).astype(jnp.bfloat16)
    weights_flat = router_weight.reshape(entries)
    returned = lax.all_to_all(unit_output, "dp", split_axis=0, concat_axis=0, tiled=True)
    unit_table = returned.reshape(2 * experts_all * quarter, width)
    lower_slot = jnp.where(entry_mine, slot_part, 0)
    route_gain = jnp.where(entry_mine, weights_flat, 0.0)
    combined = combine_routes(
        unit_table, lower_slot, experts_all * quarter, route_gain, tok_rows, topk
    )
    summed = lax.psum_scatter(combined, "tensor", scatter_dimension=1, tiled=True)
    return summed.astype(jnp.bfloat16)


def solution(mesh):
    in_specs = (
        P("dp", None),
        P(),
        P(),
        P("dp", None),
        P("dp", None),
        P("dp", None, "tensor"),
        P("dp", None, "tensor"),
        P("dp", None, "tensor"),
        P("tensor", "dp"),
        P("dp", None, "tensor"),
    )
    out_specs = P("dp", "tensor")
    return jax.shard_map(
        per_device, mesh=mesh, in_specs=in_specs, out_specs=out_specs, check_vma=False
    )
```

profile of v0, /device:TPU:0, one launch (start us, length us, event | category | flops | bytes accessed | tf_op | source)
XLA Modules:
  0.0 988.3 jit_solution(2396284120542666581)
XLA Ops:
  6.5 1.6 copy.136
  8.2 0.7 all-gather.9.cloned.1.call-update
  8.9 0.7 broadcast_multiply_fusion.1
  9.9 42.5 %all-gather.11.cloned.1.call-done = bf16[2048,2,128]{2,0,1:T(8,128)(2,1)} async-done(((bf16[256,2,128]{2,0,1:T(8,128)(2,1)}), bf16[2048,2,128]{2,0,1:T(8,128)(2,1)}) %all-gather.11.cloned.1.call-update) | async-done | bytes 1048592 | tf_op jit(solution)/shard_map/all_gather | solution.py:81
  52.5 5.7 gather_fusion.3
  58.2 7.6 broadcast_select_fusion
  65.8 10.3 %copy.137 = bf16[16,2048,128]{2,0,1:T(8,128)(2,1)} copy(bf16[16,2048,128]{2,1,0:T(8,128)(2,1)} %broadcast_select_fusion) | data formatting | bytes 16777216 | tf_op jit(solution)/shard_map/jit(_take)/select_n | solution.py:83
  76.1 4.2 gather_fusion.4
  80.4 1.7 select_bitcast_fusion
  82.7 0.5 all-gather.15.cloned.1.call-update
  84.3 0.6 dynamic_slice.11
  84.9 0.6 dynamic_slice.9
  85.4 0.6 iota_compare_fusion.3
  86.1 6.5 gather_fusion
  92.8 18.0 %reduce-window.6 = s32[64,8,128]{2,1,0:T(8,128)S(1)} reduce-window(s32[64,8,128]{2,1,0:T(8,128)S(1)} %fusion.29, s32[]{:T(128)} %constant.103.clone.1), window={size=1x1x128 pad=0_0x0_0x127_0}, to_apply=%region_0.0 | reduce-window | flops 8323072 | bytes 524292 | tf_op jit(solution)/shard_map/reduce-window
  112.8 4.3 scatter_custom_fusion
  117.1 2.5 gather_fusion.1
  119.6 2.4 fusion.16
  122.0 11.2 %psum.7 = bf16[128,32]{0,1:T(8,128)(2,1)S(1)} all-reduce(f32[128,32]{0,1:T(8,128)S(1)} %fusion.16), channel_id=1, replica_groups=mesh['dp'=8,'tensor'=4] {'tensor'}, use_global_device_ids=true, to_apply=%region_4.5 | all-reduce | flops 4096 | bytes 24576 | tf_op jit(solution)/shard_map/psum | solution.py:52
  133.3 1.5 gather_fusion.2
  135.0 0.8 reshape.478
  135.9 3.9 all-to-all-start.1
  139.7 2.2 pad_maximum_fusion
  142.0 6.1 reshape.409
  148.1 8.0 copy.130
  156.1 6.0 all-to-all-start
  162.5 3.4 fusion.44
  165.9 2.6 fusion.10
  168.5 2.6 fusion.12
  171.1 72.0 %all-to-all-done = bf16[8,16,7,2048]{3,1,2,0:T(8,128)(2,1)} async-done(((bf16[8,16,7,2048]{3,1,2,0:T(8,128)(2,1)}), bf16[8,16,7,2048]{3,1,2,0:T(8,128)(2,1)}, u32[]{:S(2)}, u32[]{:S(2)}) %all-to-all-start) | async-done | bytes 3670048 | tf_op jit(solution)/shard_map/all_to_all | solution.py:78
  243.1 103.9 %all-gather.7.cloned.1.call-done = bf16[16,2048,512]{2,1,0:T(8,128)(2,1)} async-done(((bf16[16,2048,128]{2,1,0:T(8,128)(2,1)}), bf16[16,2048,512]{2,1,0:T(8,128)(2,1)}) %all-gather.7.cloned.1.call-update) | async-done | bytes 33554448 | tf_op jit(solution)/shard_map/all_gather | solution.py:88
  347.0 19.5 %fusion.4 = f32[16,8,7,512]{3,1,2,0:T(8,128)S(1)} fusion(bf16[16,2048,512]{2,1,0:T(8,128)(2,1)} %all-gather.7.cloned.1.call-done, bf16[8,16,7,2048]{3,1,2,0:T(8,128)(2,1)} %all-to-all-done), kind=kOutput, calls=%fused_computation.11 | convolution fusion | flops 1879048192 | bytes 39059456 | tf_op jit(solution)/shard_map/slcd,ldk->slck/dot_general | solution.py:92
  366.5 188.0 %all-gather.15.cloned.1.call-done = bf16[16,2048,512]{2,1,0:T(8,128)(2,1)} async-done(((bf16[16,2048,128]{2,1,0:T(8,128)(2,1)}), bf16[16,2048,512]{2,1,0:T(8,128)(2,1)}) %all-gather.15.cloned.1.call-update) | async-done | bytes 33554448 | tf_op jit(solution)/shard_map/all_gather | solution.py:89
  554.5 23.0 %fusion.2 = f32[16,8,7,512]{3,1,2,0:T(8,128)} fusion(bf16[16,2048,512]{2,1,0:T(8,128)(2,1)} %all-gather.15.cloned.1.call-done, bf16[8,16,7,2048]{3,1,2,0:T(8,128)(2,1)} %all-to-all-done), kind=kOutput, calls=%fused_computation.9 | convolution fusion | flops 1879048192 | bytes 39059456 | tf_op jit(solution)/shard_map/slcd,ldk->slck/dot_general | solution.py:101
  577.5 7.7 fusion.15
  585.2 176.8 %all-gather.17.cloned.1.call-done = bf16[16,2048,512]{2,1,0:T(8,128)(2,1)} async-done(((bf16[16,2048,128]{2,1,0:T(8,128)(2,1)}), bf16[16,2048,512]{2,1,0:T(8,128)(2,1)}) %all-gather.17.cloned.1.call-update) | async-done | bytes 33554448 | tf_op jit(solution)/shard_map/all_gather | solution.py:109
  762.0 17.2 %convert_bitcast_fusion = bf16[8,16,7,2048]{3,0,2,1:T(8,128)(2,1)} fusion(bf16[16,2048,512]{2,1,0:T(8,128)(2,1)} %all-gather.17.cloned.1.call-done, bf16[8,16,7,512]{3,1,2,0:T(8,128)(2,1)S(1)} %fusion.15), kind=kOutput, calls=%fused_computation.16 | convolution fusion | flops 1880883200 | bytes 38141952 | tf_op jit(solution)/shard_map/slck,ldk->slcd/dot_general | solution.py:110
  779.2 5.9 copy.147
  785.0 5.5 all-to-all-start.2
  791.3 81.7 %all-to-all-done.2 = bf16[8,16,7,2048]{3,1,2,0:T(8,128)(2,1)} async-done(((bf16[8,16,7,2048]{3,1,2,0:T(8,128)(2,1)}), bf16[8,16,7,2048]{3,1,2,0:T(8,128)(2,1)}, u32[]{:S(2)}, u32[]{:S(2)}) %all-to-all-start.2) | async-done | bytes 3670048 | tf_op jit(solution)/shard_map/all_to_all | solution.py:114
  873.0 6.4 copy.148
  879.4 6.3 reshape.412
  885.7 18.9 %gather_fusion.5 = bf16[2048,2048]{1,0:T(8,128)(2,1)} fusion(bf16[896,2048]{1,0:T(8,128)(2,1)} %reshape.412, s32[2048]{0:T(1024)S(1)} %broadcast_clamp_fusion), kind=kCustom, calls=%fused_computation.5 | custom fusion | bytes 16785408 | tf_op jit(solution)/shard_map/gather | solution.py:14
  904.6 18.1 %reshape.472 = f32[128,8,2,2048]{3,2,1,0:T(2,128)} reshape(bf16[2048,2048]{1,0:T(8,128)(2,1)} %gather_fusion.5) | data formatting | bytes 25165824 | tf_op jit(solution)/shard_map/convert_element_type | solution.py:14
  922.7 26.2 %reduce_sum.28 = f32[128,8,2048]{2,1,0:T(8,128)} reduce(f32[128,8,2,2048]{3,2,1,0:T(2,128)} %reshape.472, f32[]{:T(128)} %constant.125.clone.1), dimensions={2}, to_apply=%region_5.6 | reduce | flops 2097152 | bytes 25165828 | tf_op jit(solution)/shard_map/reduce_sum | solution.py:15
  948.9 7.4 multiply_reduce_fusion
  956.4 23.2 %reduce-scatter.2.cloned.1.call-done = f32[128,512]{1,0:T(8,128)} async-done(((f32[128,2048]{1,0:T(8,128)}), f32[128,512]{1,0:T(8,128)}) %reduce-scatter.2.cloned.1.call-update) | async-done | bytes 262160 | tf_op jit(solution)/shard_map/reduce_scatter | solution.py:121
  979.5 1.6 convert_element_type.35
  (76 shorter events, 4.7 us)
Async XLA Ops:
  6.5 45.9 %all-gather.11.cloned.1.call-start = ((), (), s32[]{:S(2)}) async-start(), calls=%async_computation.6 | async-start | bytes 1179648 | tf_op jit(solution)/shard_map/all_gather | solution.py:81
  8.1 111.5 %all-gather.9.cloned.1.call-start = ((), (), s32[]{:S(2)}) async-start(), calls=%async_computation.5 | async-start | bytes 2359296 | tf_op jit(solution)/shard_map/all_gather | solution.py:45
  8.9 153.6 %all-gather.13.cloned.1.call-start = ((), (), s32[]{:S(2)}) async-start(), calls=%async_computation.7 | async-start | bytes 5242880 | tf_op jit(solution)/shard_map/all_gather | solution.py:90
  82.1 264.9 %all-gather.7.cloned.1.call-start = ((), (), s32[]{:S(2)}) async-start(), calls=%async_computation.4 | async-start | bytes 41943040 | tf_op jit(solution)/shard_map/all_gather | solution.py:88
  82.7 471.8 %all-gather.15.cloned.1.call-start = ((), (), s32[]{:S(2)}) async-start(), calls=%async_computation.8 | async-start | bytes 41943040 | tf_op jit(solution)/shard_map/all_gather | solution.py:89
  83.3 0.7 copy-start.1
  83.3 1.0 copy-start.3
  83.3 1.6 copy-start.4
  83.3 678.7 %all-gather.17.cloned.1.call-start = ((), (), s32[]{:S(2)}) async-start(), calls=%async_computation.9 | async-start | bytes 41943040 | tf_op jit(solution)/shard_map/all_gather | solution.py:109
  84.0 27.8 %copy-start.2 = (f32[128,8]{0,1:T(8,128)S(1)}, f32[128,8]{0,1:T(8,128)}, u32[]{:S(2)}) copy-start(f32[128,8]{0,1:T(8,128)} %param.14) | copy-start | bytes 12292
  84.0 28.7 %copy-start = (bf16[128,2048]{1,0:T(8,128)(2,1)S(1)}, bf16[128,2048]{1,0:T(8,128)(2,1)}, u32[]{:S(2)}) copy-start(bf16[128,2048]{1,0:T(8,128)(2,1)} %param.10) | copy-start | bytes 1572868
  135.9 20.3 %all-to-all-start.1 = ((bf16[8,2,1792]{2,1,0:T(2,128)(2,1)}), bf16[8,2,1792]{2,1,0:T(2,128)(2,1)S(1)}, u32[]{:S(2)}, u32[]{:S(2)}) async-start(bf16[8,2,1792]{2,1,0:T(2,128)(2,1)} %reshape.478), calls=%async_computation.1 | async-start | bytes 114688 | tf_op jit(solution)/shard_map/all_to_all | solution.py:79
  156.1 87.0 %all-to-all-start = ((bf16[8,16,7,2048]{3,1,2,0:T(8,128)(2,1)}), bf16[8,16,7,2048]{3,1,2,0:T(8,128)(2,1)}, u32[]{:S(2)}, u32[]{:S(2)}) async-start(bf16[8,16,7,2048]{3,1,2,0:T(8,128)(2,1)} %copy.130), calls=%async_computation | async-start | bytes 7340032 | tf_op jit(solution)/shard_map/all_to_all | solution.py:78
  785.0 88.0 %all-to-all-start.2 = ((bf16[8,16,7,2048]{3,1,2,0:T(8,128)(2,1)}), bf16[8,16,7,2048]{3,1,2,0:T(8,128)(2,1)}, u32[]{:S(2)}, u32[]{:S(2)}) async-start(bf16[8,16,7,2048]{3,1,2,0:T(8,128)(2,1)} %copy.147), calls=%async_computation.2 | async-start | bytes 7340032 | tf_op jit(solution)/shard_map/all_to_all | solution.py:114
  790.5 189.0 %reduce-scatter.2.cloned.1.call-start = ((), (), s32[]{:S(2)}) async-start(), calls=%async_computation.10 | async-start | bytes 1310720 | tf_op jit(solution)/shard_map/reduce_scatter | solution.py:121
Sparse Core Ops, SparseCore 0:
  9.5 42.8 all-gather.10
  54.5 49.8 all-gather.8
  106.0 33.4 all-gather.12
  140.9 206.0 all-gather.6
  348.4 206.0 all-gather.14
  555.9 206.0 all-gather.16
  956.5 23.0 reduce-scatter.1
where the time goes:
time: 997 us; the launch traced here: 988 us
  waiting for transfers between devices  691 us (69%)
  local copies, waits for them, and re-layouts  114 us (11%)
  other arithmetic  74.5 us (7%)
  matrix products  67.3 us (7%)
  starting transfers between devices  15.6 us (2%)
  between operations  14.8 us (1%)
  blocking collectives  11.2 us (1%)
    all_gather x1, waiting for transfers between devices, per_device(): up_piece = lax.all_gather(up_weight, 'tensor', axis=2, tiled=True)  188 us
    all_gather x1, waiting for transfers between devices, per_device(): down_whole = lax.all_gather(down_weight, 'tensor', axis=2, tiled=True)  177 us
    all_gather x1, waiting for transfers between devices, per_device(): gate_piece = lax.all_gather(gate_weight, 'tensor', axis=2, tiled=True)  104 us
    all_to_all x1, waiting for transfers between devices, per_device(): lax.all_to_all(unit_output, 'dp', split_axis=0, concat_axis=0, tiled=True)  81.7 us
    all_to_all x1, waiting for transfers between devices, per_device(): lax.all_to_all(send_rows, 'dp', split_axis=0, concat_axis=0, tiled=True)  72 us
    all_gather x1, waiting for transfers between devices, per_device(): every_table = lax.all_gather(adapter_output_maps, 'dp', axis=0, tiled=True)  42.5 us
    reduce_sum x1, other arithmetic, combine_routes(): summed_pair = jnp.sum(pair_rows, axis=2)  26.2 us
    reduce_scatter x1, waiting for transfers between devices, per_device(): lax.psum_scatter(combined, 'tensor', scatter_dimension=1, tiled=True)  23.2 us
  transfers between devices with their start and end apart: 10, of which 7 were waited for; matrix products, arithmetic and copies ran while one was open for 15% of the time, Pallas kernels for 0%

commit v1 on v0

--- a/solution.py
+++ b/solution.py
@@ -5,6 +5,30 @@
 
 ADAPTER_RANK = 16
 CAP = 28
+
+
+def ring_apply(x, axis, dim, work, out_dim):
+    size, here, width = (lax.axis_size(axis), lax.axis_index(axis), x.shape[dim])
+    right = [(i, (i + 1) % size) for i in range(size)]
+    left = [(b, a) for a, b in right]
+    lower, upper = (lax.ppermute(x, axis, right), lax.ppermute(x, axis, left))
+    made = work(x, here * width)
+    length = made.shape[out_dim]
+    out = jnp.zeros((*made.shape[:out_dim], size * length, *made.shape[out_dim + 1 :]), made.dtype)
+
+    def put(out, made, owner):
+        return lax.dynamic_update_slice_in_dim(out, made, owner * length, axis=out_dim)
+
+    out = put(out, made, here)
+    for hop in range(1, size // 2 + 1):
+        below, above = ((here - hop) % size, (here + hop) % size)
+        carried = (lower, upper)
+        if hop < size // 2:
+            lower, upper = (lax.ppermute(lower, axis, right), lax.ppermute(upper, axis, left))
+        out = put(out, work(carried[0], below * width), below)
+        if 2 * hop < size:
+            out = put(out, work(carried[1], above * width), above)
+    return out
 
 
 def combine_routes(unit_table, lower_slot, shift_half, route_gain, tok_rows, topk):
@@ -85,12 +109,17 @@
         request_adapter[:, None] * double_rank + jnp.arange(double_rank)[None, :]
     ).reshape(dp_count * double_rank)
     source_tables = jnp.take(half_tables, source_rows, axis=1)
-    gate_piece = lax.all_gather(gate_weight, "tensor", axis=2, tiled=True)
     up_piece = lax.all_gather(up_weight, "tensor", axis=2, tiled=True)
     table_piece = lax.all_gather(source_tables, "tensor", axis=2, tiled=True)
     table_split = table_piece.reshape(units_local, dp_count, double_rank, table_piece.shape[2])
-    gate_term = jnp.einsum(
-        "slcd,ldk->slck", recv_rows, gate_piece, preferred_element_type=jnp.float32
+    gate_term = ring_apply(
+        gate_weight,
+        "tensor",
+        2,
+        lambda shard, offset: jnp.einsum(
+            "slcd,ldk->slck", recv_rows, shard, preferred_element_type=jnp.float32
+        ),
+        3,
     )
     gate_term = gate_term + jnp.einsum(
         "slcj,lsjk->slck",

time: 997 us -> 981 us (0.984)
  waiting for transfers between devices: 691 us -> 529 us
  blocking collectives: 11.2 us -> 140 us
  matrix products: 67.3 us -> 90.6 us
    ppermute x0 -> x3, waiting for transfers between devices: none -> 229 us  [the longest x2 229 us: ring_apply(): lower, upper = (lax.ppermute(x, axis, right), lax.ppermute(x, axis, left))]
    all_gather x1, waiting for transfers between devices: 188 us -> 0.02 us  [per_device(): up_piece = lax.all_gather(up_weight, 'tensor', axis=2, tiled=True)]
    psum x1, blocking collectives: 11.2 us -> 140 us  [per_device(): low_rank = lax.psum(partial_z, 'tensor').astype(jnp.bfloat16)]
    all_gather x1, waiting for transfers between devices: 177 us -> 69.4 us  [per_device(): down_whole = lax.all_gather(down_weight, 'tensor', axis=2, tiled=True)]
    all_gather x1 -> x0, waiting for transfers between devices: 104 us -> none  [per_device(): gate_piece = lax.all_gather(gate_weight, 'tensor', axis=2, tiled=True)]
    dot_general x1 -> x4, matrix products: 19.5 us -> 43.8 us  [per_device(): jnp.einsum('slcd,ldk->slck', recv_rows, shard, preferred_element_type=jnp...]
  transfers between devices with their start and end apart: 10 -> 12, of which waited for: 7 -> 6; matrix products, arithmetic and copies ran while one was open for 15% -> 17% of each run, Pallas kernels for 0% -> 0%
where the time goes in v1:
time: 981 us; the launch traced here: 972 us
  waiting for transfers between devices  529 us (54%)
  blocking collectives  140 us (14%)
  local copies, waits for them, and re-layouts  115 us (12%)
  matrix products  90.6 us (9%)
  other arithmetic  66.8 us (7%)
  starting transfers between devices  15.1 us (2%)
  between operations  15.1 us (2%)
    ppermute x2, waiting for transfers between devices, ring_apply(): lower, upper = (lax.ppermute(x, axis, right), lax.ppermute(x, axis, left))  229 us
    psum x1, blocking collectives, per_device(): low_rank = lax.psum(partial_z, 'tensor').astype(jnp.bfloat16)  140 us
    all_to_all x1, waiting for transfers between devices, per_device(): lax.all_to_all(unit_output, 'dp', split_axis=0, concat_axis=0, tiled=True)  81.7 us
    all_to_all x1, waiting for transfers between devices, per_device(): lax.all_to_all(send_rows, 'dp', split_axis=0, concat_axis=0, tiled=True)  81 us
    all_gather x1, waiting for transfers between devices, per_device(): down_whole = lax.all_gather(down_weight, 'tensor', axis=2, tiled=True)  69.4 us
    dot_general x4, matrix products, per_device(): jnp.einsum('slcd,ldk->slck', recv_rows, shard, preferred_element_type=jnp...  43.8 us
    all_gather x1, waiting for transfers between devices, per_device(): every_table = lax.all_gather(adapter_output_maps, 'dp', axis=0, tiled=True)  42.5 us
    reduce_sum x1, other arithmetic, combine_routes(): summed_pair = jnp.sum(pair_rows, axis=2)  26.2 us
  transfers between devices with their start and end apart: 12, of which 6 were waited for; matrix products, arithmetic and copies ran while one was open for 17% of the time, Pallas kernels for 0%

profile of v1, /device:TPU:0, one launch (start us, length us, event | category | flops | bytes accessed | tf_op | source)
XLA Modules:
  0.0 971.9 jit_solution(5759900859813038929)
XLA Ops:
  6.5 1.6 copy.138
  8.2 0.7 all-gather.6.cloned.1.call-update
  8.9 0.7 broadcast_multiply_fusion.1
  9.9 42.5 %all-gather.8.cloned.1.call-done = bf16[2048,2,128]{2,0,1:T(8,128)(2,1)} async-done(((bf16[256,2,128]{2,0,1:T(8,128)(2,1)}), bf16[2048,2,128]{2,0,1:T(8,128)(2,1)}) %all-gather.8.cloned.1.call-update) | async-done | bytes 1048592 | tf_op jit(solution)/shard_map/all_gather | solution.py:105
  52.5 5.7 gather_fusion.3
  58.2 7.6 broadcast_select_fusion
  65.8 10.3 %copy.139 = bf16[16,2048,128]{2,0,1:T(8,128)(2,1)} copy(bf16[16,2048,128]{2,1,0:T(8,128)(2,1)} %broadcast_select_fusion) | data formatting | bytes 16777216 | tf_op jit(solution)/shard_map/jit(_take)/select_n | solution.py:107
  76.1 4.2 gather_fusion.4
  80.4 1.7 select_bitcast_fusion
  84.3 0.6 dynamic_slice.9
  84.9 0.6 iota_compare_fusion.3
  85.5 6.5 gather_fusion
  92.2 18.0 %reduce-window.6 = s32[64,8,128]{2,1,0:T(8,128)S(1)} reduce-window(s32[64,8,128]{2,1,0:T(8,128)S(1)} %fusion.60, s32[]{:T(128)} %constant.128.clone.1), window={size=1x1x128 pad=0_0x0_0x127_0}, to_apply=%region_0.0 | reduce-window | flops 8323072 | bytes 524292 | tf_op jit(solution)/shard_map/reduce-window
  111.5 4.3 scatter_custom_fusion
  115.9 2.5 gather_fusion.1
  119.0 2.4 fusion.47
  121.5 140.2 %psum.7 = bf16[128,32]{0,1:T(8,128)(2,1)S(1)} all-reduce(f32[128,32]{0,1:T(8,128)S(1)} %fusion.47), channel_id=1, replica_groups=mesh['dp'=8,'tensor'=4] {'tensor'}, use_global_device_ids=true, to_apply=%region_4.5 | all-reduce | flops 4096 | bytes 24576 | tf_op jit(solution)/shard_map/psum | solution.py:76
  261.8 1.5 gather_fusion.2
  263.5 0.8 reshape.481
  264.3 3.6 all-to-all-start.1
  267.9 2.3 pad_maximum_fusion
  270.2 6.0 reshape.409
  276.2 6.6 copy.126
  282.7 6.0 all-to-all-start
  289.4 0.8 fusion.76
  290.1 81.0 %all-to-all-done = bf16[8,16,7,2048]{3,1,2,0:T(8,128)(2,1)} async-done(((bf16[8,16,7,2048]{3,1,2,0:T(8,128)(2,1)}), bf16[8,16,7,2048]{3,1,2,0:T(8,128)(2,1)}, u32[]{:S(2)}, u32[]{:S(2)}) %all-to-all-start) | async-done | bytes 3670048 | tf_op jit(solution)/shard_map/all_to_all | solution.py:102
  371.1 8.8 fusion.27
  380.4 4.0 fusion.75
  384.4 2.6 fusion.19
  387.0 8.8 fusion.32
  395.9 229.0 %collective-permute-done.1 = bf16[16,2048,128]{2,1,0:T(8,128)(2,1)} collective-permute-done((bf16[16,2048,128]{2,1,0:T(8,128)(2,1)}, bf16[16,2048,128]{2,1,0:T(8,128)(2,1)}, u32[]{:S(2)}, u32[]{:S(2)}) %collective-permute-start.1) | collective-permute-done | bytes 8388640 | tf_op jit(solution)/shard_map/ppermute | solution.py:14
  625.0 17.5 %fusion.37 = f32[8,16,7,128]{3,0,2,1:T(8,128)S(1)} fusion(bf16[16,2048,128]{2,1,0:T(8,128)(2,1)} %collective-permute-done.1, bf16[8,16,7,2048]{3,1,2,0:T(8,128)(2,1)} %all-to-all-done), kind=kOutput, calls=%fused_computation.37 | convolution fusion | flops 469762048 | bytes 12517376 | tf_op jit(solution)/shard_map/slcd,ldk->slck/dot_general | solution.py:119
  642.7 8.8 fusion.42
  651.7 20.1 %fusion.2 = f32[16,8,7,512]{3,2,0,1:T(8,128)} fusion(bf16[16,2048,512]{2,1,0:T(8,128)(2,1)} %all-gather.12.cloned.1.call-done, bf16[8,16,7,2048]{3,1,2,0:T(8,128)(2,1)} %all-to-all-done), kind=kOutput, calls=%fused_computation.9 | convolution fusion | flops 1879048192 | bytes 39059456 | tf_op jit(solution)/shard_map/slcd,ldk->slck/dot_general | solution.py:130
  671.8 4.7 fusion.24
  676.5 69.4 %all-gather.14.cloned.1.call-done = bf16[16,2048,512]{2,1,0:T(8,128)(2,1)} async-done(((bf16[16,2048,128]{2,1,0:T(8,128)(2,1)}), bf16[16,2048,512]{2,1,0:T(8,128)(2,1)}) %all-gather.14.cloned.1.call-update) | async-done | bytes 33554448 | tf_op jit(solution)/shard_map/all_gather | solution.py:138
  745.9 17.0 %convert_bitcast_fusion = bf16[8,16,7,2048]{3,0,2,1:T(8,128)(2,1)} fusion(bf16[16,2048,512]{2,1,0:T(8,128)(2,1)} %all-gather.14.cloned.1.call-done, bf16[8,16,7,512]{3,2,1,0:T(8,128)(2,1)S(1)} %fusion.24), kind=kOutput, calls=%fused_computation.23 | convolution fusion | flops 1880883200 | bytes 38141952 | tf_op jit(solution)/shard_map/slck,ldk->slcd/dot_general | solution.py:139
  762.9 5.9 copy.146
  768.7 4.5 all-to-all-start.2
  774.3 81.7 %all-to-all-done.2 = bf16[8,16,7,2048]{3,1,2,0:T(8,128)(2,1)} async-done(((bf16[8,16,7,2048]{3,1,2,0:T(8,128)(2,1)}), bf16[8,16,7,2048]{3,1,2,0:T(8,128)(2,1)}, u32[]{:S(2)}, u32[]{:S(2)}) %all-to-all-start.2) | async-done | bytes 3670048 | tf_op jit(solution)/shard_map/all_to_all | solution.py:143
  855.9 6.4 copy.147
  862.3 6.1 reshape.412
  868.4 18.9 %gather_fusion.5 = bf16[2048,2048]{1,0:T(8,128)(2,1)} fusion(bf16[896,2048]{1,0:T(8,128)(2,1)} %reshape.412, s32[2048]{0:T(1024)S(1)} %broadcast_clamp_fusion), kind=kCustom, calls=%fused_computation.5 | custom fusion | bytes 16785408 | tf_op jit(solution)/shard_map/gather | solution.py:38
  887.3 18.1 %reshape.472 = f32[128,8,2,2048]{3,2,1,0:T(2,128)} reshape(bf16[2048,2048]{1,0:T(8,128)(2,1)} %gather_fusion.5) | data formatting | bytes 25165824 | tf_op jit(solution)/shard_map/convert_element_type | solution.py:38
  905.4 26.2 %reduce_sum.28 = f32[128,8,2048]{2,1,0:T(8,128)} reduce(f32[128,8,2,2048]{3,2,1,0:T(2,128)} %reshape.472, f32[]{:T(128)} %constant.123.clone.1), dimensions={2}, to_apply=%region_5.6 | reduce | flops 2097152 | bytes 25165828 | tf_op jit(solution)/shard_map/reduce_sum | solution.py:39
  931.6 7.4 multiply_reduce_fusion
  939.0 24.0 %reduce-scatter.2.cloned.1.call-done = f32[128,512]{1,0:T(8,128)} async-done(((f32[128,2048]{1,0:T(8,128)}), f32[128,512]{1,0:T(8,128)}) %reduce-scatter.2.cloned.1.call-update) | async-done | bytes 262160 | tf_op jit(solution)/shard_map/reduce_scatter | solution.py:150
  963.0 1.6 convert_element_type.35
  (86 shorter events, 6.9 us)
Async XLA Ops:
  6.5 45.9 %all-gather.8.cloned.1.call-start = ((), (), s32[]{:S(2)}) async-start(), calls=%async_computation.5 | async-start | bytes 1179648 | tf_op jit(solution)/shard_map/all_gather | solution.py:105
  8.1 110.9 %all-gather.6.cloned.1.call-start = ((), (), s32[]{:S(2)}) async-start(), calls=%async_computation.4 | async-start | bytes 2359296 | tf_op jit(solution)/shard_map/all_gather | solution.py:69
  8.9 371.5 %all-gather.10.cloned.1.call-start = ((), (), s32[]{:S(2)}) async-start(), calls=%async_computation.6 | async-start | bytes 5242880 | tf_op jit(solution)/shard_map/all_gather | solution.py:113
  82.1 569.6 %all-gather.12.cloned.1.call-start = ((), (), s32[]{:S(2)}) async-start(), calls=%async_computation.7 | async-start | bytes 41943040 | tf_op jit(solution)/shard_map/all_gather | solution.py:112
  82.7 0.7 copy-start.1
  82.7 1.0 copy-start.3
  82.7 1.6 copy-start.4
  82.7 663.2 %all-gather.14.cloned.1.call-start = ((), (), s32[]{:S(2)}) async-start(), calls=%async_computation.8 | async-start | bytes 41943040 | tf_op jit(solution)/shard_map/all_gather | solution.py:138
  83.3 27.8 %copy-start.2 = (f32[128,8]{0,1:T(8,128)S(1)}, f32[128,8]{0,1:T(8,128)}, u32[]{:S(2)}) copy-start(f32[128,8]{0,1:T(8,128)} %param.14) | copy-start | bytes 12292
  83.3 28.1 %copy-start = (bf16[128,2048]{1,0:T(8,128)(2,1)S(1)}, bf16[128,2048]{1,0:T(8,128)(2,1)}, u32[]{:S(2)}) copy-start(bf16[128,2048]{1,0:T(8,128)(2,1)} %param.10) | copy-start | bytes 1572868
  83.3 205.4 %collective-permute-start = (bf16[16,2048,128]{2,1,0:T(8,128)(2,1)}, bf16[16,2048,128]{2,1,0:T(8,128)(2,1)}, u32[]{:S(2)}, u32[]{:S(2)}) collective-permute-start(bf16[16,2048,128]{2,1,0:T(8,128)(2,1)} %param.15), channel_id=1, source_target_pairs={{0,1},{1,2},{2,3},{3,0},{4,5},{5,6},{6,7},{7,4},{8,9},{9,10},{10,1... | collective-permute-start | bytes 25165832 | tf_op jit(solution)/shard_map/ppermute | solution.py:14
  264.3 18.4 %all-to-all-start.1 = ((bf16[8,2,1792]{2,1,0:T(2,128)(2,1)}), bf16[8,2,1792]{2,1,0:T(2,128)(2,1)S(1)}, u32[]{:S(2)}, u32[]{:S(2)}) async-start(bf16[8,2,1792]{2,1,0:T(2,128)(2,1)} %reshape.481), calls=%async_computation.1 | async-start | bytes 114688 | tf_op jit(solution)/shard_map/all_to_all | solution.py:103
  282.7 88.4 %all-to-all-start = ((bf16[8,16,7,2048]{3,1,2,0:T(8,128)(2,1)}), bf16[8,16,7,2048]{3,1,2,0:T(8,128)(2,1)}, u32[]{:S(2)}, u32[]{:S(2)}) async-start(bf16[8,16,7,2048]{3,1,2,0:T(8,128)(2,1)} %copy.126), calls=%async_computation | async-start | bytes 7340032 | tf_op jit(solution)/shard_map/all_to_all | solution.py:102
  288.7 336.3 %collective-permute-start.1 = (bf16[16,2048,128]{2,1,0:T(8,128)(2,1)}, bf16[16,2048,128]{2,1,0:T(8,128)(2,1)}, u32[]{:S(2)}, u32[]{:S(2)}) collective-permute-start(bf16[16,2048,128]{2,1,0:T(8,128)(2,1)} %param.15), channel_id=1, source_target_pairs={{1,0},{2,1},{3,2},{0,3},{5,4},{6,5},{7,6},{4,7},{9,8},{10,9},{11,1... | collective-permute-start | bytes 25165832 | tf_op jit(solution)/shard_map/ppermute | solution.py:14
  288.7 353.9 %collective-permute-start.2 = (bf16[16,2048,128]{2,1,0:T(8,128)(2,1)}, bf16[16,2048,128]{2,1,0:T(8,128)(2,1)}, u32[]{:S(2)}, u32[]{:S(2)}) collective-permute-start(bf16[16,2048,128]{2,1,0:T(8,128)(2,1)} %collective-permute-done), channel_id=1, source_target_pairs={{0,1},{1,2},{2,3},{3,0},{4,5},{5,6},{6,7},{7,4},{8,9},{9,10},{10,1... | collective-permute-start | bytes 25165832 | tf_op jit(solution)/shard_map/ppermute | solution.py:27
  768.7 87.2 %all-to-all-start.2 = ((bf16[8,16,7,2048]{3,1,2,0:T(8,128)(2,1)}), bf16[8,16,7,2048]{3,1,2,0:T(8,128)(2,1)}, u32[]{:S(2)}, u32[]{:S(2)}) async-start(bf16[8,16,7,2048]{3,1,2,0:T(8,128)(2,1)} %copy.146), calls=%async_computation.2 | async-start | bytes 7340032 | tf_op jit(solution)/shard_map/all_to_all | solution.py:143
  773.3 189.7 %reduce-scatter.2.cloned.1.call-start = ((), (), s32[]{:S(2)}) async-start(), calls=%async_computation.9 | async-start | bytes 1310720 | tf_op jit(solution)/shard_map/reduce_scatter | solution.py:150
Sparse Core Ops, SparseCore 0:
  9.5 42.8 all-gather.7
  54.5 49.8 all-gather.5
  105.9 44.6 all-gather.9
  152.0 320.2 all-gather.11
  473.7 272.1 all-gather.13
  939.1 23.8 reduce-scatter.1
